TPU v7x, 32 devices: a whole 2x2x4 slice. The times are simulated.
32 devices in a mesh: lat: 4 (over y, core), blk: 4 (over z), probe: 2 (over x).
Axes of the slice: x: 2, y: 2, z: 4, core: 2. Of those that a mesh axis runs over, the one named last changes fastest.
Arguments:
- probes_in: bfloat16 [64, 2, 640, 640], P('probe', None, ('lat', 'blk')), may hold values from -1.5 to 1.5
- root_spectrum: float32 [640], replicated, may hold values from 0.2 to 3, as said below
- order_slots: int32 [640], replicated, may hold values from 0 to 639, as said below
- legendre: bfloat16 [640, 640, 1280], P(None, ('lat', 'blk')), as said below
- weight: float32 [1280, 2560], P(('lat', 'blk')), may hold values from 0.2 to 5
- beta: float32 [64], P('probe'), may hold values from 0.5 to 2
Outputs:
- matvec: float32 [64, 2, 640, 640], P('probe', None, ('lat', 'blk'))
- gradient: float32 [1280, 2560], P(('lat', 'blk'), 'probe')
Inputs may be any that keep to these rules, and one draw needn't show every extreme that they name: order_slots is a permutation of 0 to 639, and slots 2k and 2k + 1 hold orders that sum to 639. legendre[l, s, j] is the orthonormal associated Legendre function (no Condon-Shortley sign) of degree l and order order_slots[s] at cos(theta_j), zero for l below the order, rounded to bfloat16. root_spectrum is drawn afresh for each degree.
All inputs are finite; a program needn't handle non-finite values.
Results may differ from a plain program's by a relative error of at most 0.0031.
Values may be sent and summed in bfloat16 or wider, within the bound.
No kernel may reach another device: no remote copies, remote signals or barrier semaphores. Data moves between devices by JAX's collectives and lax.ppermute only.
A program may use at most 320 MiB of HBM per device.

v0:
```python
import functools
import math

import jax
import jax.numpy as jnp
from jax import lax
from jax.experimental import pallas as pl
from jax.experimental.pallas import tpu as pltpu
from jax.sharding import PartitionSpec as P

GROUP = 8
DEPTH = 128
CHUNK = 16
PART = 8
TILE = 256
VMEM_LIMIT = 60 * 2**20


def fourier_tables(orders, lon_count):
    longitude = jnp.arange(lon_count, dtype=jnp.int32)
    phase_idx = orders[:, None] * longitude[None, :] % lon_count
    angle = phase_idx.astype(jnp.float32) * (2.0 * math.pi / lon_count)
    twiddle = jnp.stack([jnp.cos(angle), jnp.sin(angle)])
    upper = twiddle.astype(jnp.bfloat16)
    lower = (twiddle - upper.astype(jnp.float32)).astype(jnp.bfloat16)
    return (upper, lower)


def cycle_work(spectra, inverse_tables, forward_tables, area, weight):
    grid_field = jnp.einsum(
        "pcmj,cmx->pjx", spectra, inverse_tables[0], preferred_element_type=jnp.float32
    )
    grid_field = grid_field + jnp.einsum(
        "pcmj,cmx->pjx", spectra, inverse_tables[1], preferred_element_type=jnp.float32
    )
    squares = grid_field * grid_field
    weighted = (area[None, :, None] * weight[None] * grid_field).astype(jnp.bfloat16)
    analysed = jnp.einsum(
        "pjx,cmx->pcmj", weighted, forward_tables[0], preferred_element_type=jnp.float32
    )
    analysed = analysed + jnp.einsum(
        "pjx,cmx->pcmj", weighted, forward_tables[1], preferred_element_type=jnp.float32
    )
    return (squares, analysed.astype(jnp.bfloat16))


def plain_body(probes_in, root_spectrum, order_slots, legendre, weight, beta):
    groups = lax.axis_size(("lat", "blk"))
    my_index = lax.axis_index(("lat", "blk"))
    cycle_count = weight.shape[0]
    lon_count = weight.shape[1]
    all_cycles = cycle_count * groups
    scaled = (probes_in.astype(jnp.float32) * root_spectrum).astype(jnp.bfloat16)
    spectra = jnp.einsum(
        "pcml,lmj->pcmj", scaled, legendre, preferred_element_type=jnp.float32
    ).astype(jnp.bfloat16)
    cycle_index = (my_index * cycle_count + jnp.arange(cycle_count, dtype=jnp.int32)).astype(
        jnp.float32
    )
    local_sines = jnp.sin(math.pi * (cycle_index + 0.5) / all_cycles)
    area = 2.0 * math.pi / lon_count * (math.pi / all_cycles) * local_sines
    forward_tables = fourier_tables(order_slots, lon_count)
    squares, analysed = cycle_work(
        lax.all_to_all(spectra, ("lat", "blk"), split_axis=3, concat_axis=2, tiled=True),
        forward_tables,
        forward_tables,
        area,
        weight,
    )
    returned = lax.all_to_all(analysed, ("lat", "blk"), split_axis=2, concat_axis=3, tiled=True)
    matvec = (
        jnp.einsum("pcmj,lmj->pcml", returned, legendre, preferred_element_type=jnp.float32)
        * root_spectrum
    )
    grad_terms = jnp.einsum("pjx,p->jx", squares, beta) * area[:, None]
    gradient = lax.psum_scatter(grad_terms, "probe", scatter_dimension=1, tiled=True)
    return (matvec, gradient)


def dot(a, b, dims=((1,), (0,))):
    return lax.dot_general(a, b, (dims, ((), ())), preferred_element_type=jnp.float32)


def split(x):
    upper = x.astype(jnp.bfloat16)
    return upper, (x - upper.astype(jnp.float32)).astype(jnp.bfloat16)


LANES = 128


def every(slot, count):
    return pl.ds(slot, count, stride=GROUP)


def tiles(ref):
    return range(ref.shape[0])


def put(ref, rows, value):
    for t in tiles(ref):
        ref[t, rows, :] = value[:, t * LANES : (t + 1) * LANES]


def take(ref, rows):
    return jnp.concatenate([ref[t, rows, :] for t in tiles(ref)], axis=-1)


def spread_rows(tbl_ref, wide):
    @pl.loop(0, tbl_ref.shape[0] * 2 // DEPTH)
    def _(step):
        some = pl.ds(step * (DEPTH // 2), DEPTH // 2)
        for t in tiles(wide):
            piece = tbl_ref[some, :, :, t * LANES : (t + 1) * LANES].astype(jnp.float32)
            wide[t, pl.ds(step * (DEPTH * GROUP), DEPTH * GROUP)] = piece.reshape(
                DEPTH * GROUP, LANES
            )


def visit(orders_ref, group, turn, pair, steps):
    first = orders_ref[group * GROUP + 2 * pair] // DEPTH
    mine = turn < steps - first
    slot = 2 * pair + jnp.where(mine, 0, 1)
    return slot, jnp.where(mine, first + turn, turn - 1)


def even_degree(shape):
    return lax.broadcasted_iota(jnp.int32, shape, 1) % 2 == 0


def synth_kernel(orders_ref, x_ref, root_ref, tbl_ref, sign_ref, out_ref, xs, wide, acc, ns, ss):
    group = pl.program_id(0)
    chunk = x_ref.shape[0]
    cycles = out_ref.shape[3] // chunk
    half = out_ref.shape[0] // 2
    rows = chunk * 2
    scaled = (x_ref[...].astype(jnp.float32) * root_ref[...]).astype(jnp.bfloat16)
    put(xs, slice(None), scaled.astype(jnp.float32).reshape(rows * GROUP, scaled.shape[-1]))
    acc[...] = jnp.zeros_like(acc)

    spread_rows(tbl_ref, wide)
    steps = tbl_ref.shape[0] * 2 // DEPTH

    @pl.loop(0, steps + 1)
    def _(turn):
        for pair in range(GROUP // 2):
            slot, step = visit(orders_ref, group, turn, pair, steps)
            x = xs[step, every(slot, rows), :]
            even = even_degree(x.shape)
            x = jnp.concatenate([jnp.where(even, x, 0.0), jnp.where(even, 0.0, x)], axis=0)
            table = take(wide, every(step * (DEPTH * GROUP) + slot, DEPTH)).astype(jnp.bfloat16)
            acc[slot] += dot(x.astype(jnp.bfloat16), table)

    for slot in range(GROUP):
        even, odd = acc[slot, :rows], acc[slot, rows:]
        put(ns, every(slot, rows), even + odd)
        put(ss, every(slot, rows), even - odd)
    for c in range(2):
        north, south = [], []
        for p in range(chunk):
            place = pl.ds((2 * p + c) * GROUP, GROUP)
            north.append(take(ns, place))
            south.append(take(ss, place) * sign_ref[...])
        for d in range(half):
            for source, place in ((north, d), (south, 2 * half - 1 - d)):
                pieces = [piece[:, d * cycles : (d + 1) * cycles] for piece in source]
                out_ref[place, c] = jnp.concatenate(pieces, axis=-1).astype(jnp.bfloat16)


def analysis_kernel(*refs):
    orders_ref, q_ref, root_ref, tbl_ref, sign_ref = refs[:5]
    out_ref, plus, minus, wide, held, outs = refs[-6:]
    group = pl.program_id(0)
    chunk = out_ref.shape[0]
    cycles = q_ref.shape[3] // chunk
    half = q_ref.shape[0] // 2
    rows = chunk * 2

    for c in range(2):
        blocks = [q_ref[d, c].astype(jnp.float32) for d in range(2 * half)]
        for p in range(chunk):
            cut = slice(p * cycles, (p + 1) * cycles)
            north = jnp.concatenate([blocks[d][:, cut] for d in range(half)], axis=-1)
            other = [blocks[2 * half - 1 - d][:, cut] for d in range(half)]
            south = jnp.concatenate(other, axis=-1) * sign_ref[...]
            place = pl.ds((2 * p + c) * GROUP, GROUP)
            put(plus, place, north + south)
            put(minus, place, north - south)
    for slot in range(GROUP):
        both = [take(ref, every(slot, rows)) for ref in (plus, minus)]
        upper, lower = split(jnp.concatenate(both, axis=0))
        held[slot, : 2 * rows] = upper
        held[slot, 2 * rows :] = lower
    outs[...] = jnp.zeros_like(outs)

    spread_rows(tbl_ref, wide)
    steps = tbl_ref.shape[0] * 2 // DEPTH

    @pl.loop(0, steps + 1)
    def _(turn):
        for pair in range(GROUP // 2):
            slot, step = visit(orders_ref, group, turn, pair, steps)
            now = pl.ds(pl.multiple_of(step * DEPTH, DEPTH), DEPTH)
            table = take(wide, every(step * (DEPTH * GROUP) + slot, DEPTH)).astype(jnp.bfloat16)
            both = dot(held[slot], table, ((1,), (1,)))
            both = both[: 2 * rows] + both[2 * rows :]
            even = even_degree((rows, DEPTH))
            chosen = jnp.where(even, both[:rows], both[rows:])
            outs[step, every(slot, rows), :] = chosen * root_ref[:, now]

    for t in tiles(outs):
        cut = slice(t * LANES, (t + 1) * LANES)
        out_ref[:, :, :, cut] = outs[t].reshape(chunk, 2, GROUP, LANES)


def fourier_kernel(*refs, first):
    r_ref, ahead_cos, ahead_sin, back_cos, back_sin, w_low, w_high, turn_ref, beta_ref = refs[:9]
    out_ref, g_low, g_high, rc, rs, acc_c, acc_s, middle = refs[-8:]
    old_low, old_high = (None, None) if first else refs[9:11]
    step, part = pl.program_id(0), pl.program_id(1)
    sources, _, slots, _ = r_ref.shape
    tile, lanes = g_low.shape
    count = acc_c.shape[1]
    mine = pl.ds(pl.multiple_of(part * lanes, LANES), lanes)

    @pl.when(step == 0)
    def _():
        for pair in range(sources // 2):
            for c, place in ((0, rc), (1, rs)):
                both = [r_ref[2 * pair + i, c, :, mine].astype(jnp.float32) for i in range(2)]
                place[part, pl.ds(2 * slots * pair, 2 * slots)] = jnp.concatenate(
                    both, axis=0
                ).astype(jnp.bfloat16)
        turned = turn_ref[...] * rc[part].astype(jnp.float32)
        mid = jnp.sum(turned, axis=0, keepdims=True)
        middle[part] = mid
        w_mid = (w_high[pl.ds(0, 1), :] * mid).astype(jnp.bfloat16).astype(jnp.float32)
        acc_c[part] = turn_ref[...] * w_mid
        acc_s[part] = jnp.zeros_like(acc_s[part])

    c_part = dot(ahead_cos[0], rc[part])
    c_part = c_part[:tile] + c_part[tile:]
    s_part = dot(ahead_sin[0], rs[part])
    s_part = s_part[:tile] + s_part[tile:]
    low = c_part + s_part
    row = lax.broadcasted_iota(jnp.int32, low.shape, 0) + step * tile
    high = jnp.where(row == 0, middle[part], c_part - s_part)
    beta = beta_ref[:, mine]
    low_sq = beta * (low * low)
    high_sq = beta * (high * high)

    @pl.when(part == 0)
    def _():
        g_low[...] = low_sq if first else old_low[...] + low_sq
        g_high[...] = high_sq if first else old_high[...] + high_sq

    @pl.when(part > 0)
    def _():
        g_low[...] += low_sq
        g_high[...] += high_sq

    low = (w_low[...] * low).astype(jnp.bfloat16).astype(jnp.float32)
    high = jnp.where(row == 0, 0.0, w_high[...] * high).astype(jnp.bfloat16).astype(jnp.float32)
    for folded, back, acc in ((low + high, back_cos, acc_c), (low - high, back_sin, acc_s)):
        upper, lower = split(folded)
        both = dot(back[...], upper)
        acc[part] += both[:count] + both[count:] + dot(back[pl.ds(0, count), :], lower)

    @pl.when(step == pl.num_programs(0) - 1)
    def _():
        for d in range(sources):
            for c, acc in ((0, acc_c), (1, acc_s)):
                out_ref[d, c, :, mine] = acc[part, pl.ds(slots * d, slots)].astype(jnp.bfloat16)


def half_tables(orders, lon_count):
    half = lon_count // 2

    def trig(points):
        idx = orders[:, None] * points[None, :] % lon_count
        angle = idx.astype(jnp.float32) * (2.0 * math.pi / lon_count)
        return lax.optimization_barrier((jnp.cos(angle), jnp.sin(angle)))

    def joined(parts, fine, shape, axes):
        (ca, sa), (cb, sb) = parts
        ca, sa = (t[axes[0]] for t in (ca, sa))
        cb, sb = (t[axes[1]] for t in (cb, sb))
        cosine = (ca * cb - sa * sb).reshape(shape)
        sine = (sa * cb + ca * sb).reshape(shape)
        return split(cosine) + split(sine)

    count = orders.shape[0]
    fine = 128
    coarse_points = jnp.arange(half // fine, dtype=jnp.int32) * fine
    fine_points = jnp.arange(fine, dtype=jnp.int32)
    coarse, small = trig(coarse_points), trig(fine_points)
    every = slice(None)
    back = joined(
        (coarse, small), fine, (count, half), ((every, every, None), (every, None, every))
    )
    coarse_t = tuple(t.T for t in coarse)
    small_t = tuple(t.T for t in small)
    ahead = joined(
        (coarse_t, small_t), fine, (half, count), ((every, None, every), (None, every, every))
    )
    tiled = [t.reshape(half // TILE, TILE, count) for t in ahead]
    ahead = [jnp.concatenate(tiled[i : i + 2], axis=1) for i in (0, 2)]
    back = [jnp.concatenate(back[i : i + 2], axis=0) for i in (0, 2)]
    return ahead, back


def fast_body(probes_in, root_spectrum, order_slots, legendre, weight, beta):
    axes = ("lat", "blk")
    groups = lax.axis_size(axes)
    my_index = lax.axis_index(axes)
    cycles, lon_count = weight.shape
    half_lon = lon_count // 2
    all_cycles = cycles * groups
    half_cycles = all_cycles // 2
    degrees, slots = legendre.shape[:2]
    orders_count = order_slots.shape[0]
    probes = probes_in.shape[0]
    chunks = probes // CHUNK
    lanes = CHUNK * cycles
    part_lanes = PART * cycles
    parts = CHUNK // PART
    south = my_index >= groups // 2
    params = functools.partial(pltpu.CompilerParams, vmem_limit_bytes=VMEM_LIMIT)
    f32, bf16 = jnp.float32, jnp.bfloat16

    my_orders = lax.dynamic_slice_in_dim(order_slots, my_index * slots, slots)
    sign = (1 - 2 * (my_orders % 2)).astype(f32)
    sign = jnp.broadcast_to(sign[:, None], (slots, half_cycles))
    root = root_spectrum[None, :]
    table = legendre.reshape(degrees // 2, 2, slots, all_cycles)
    rows = CHUNK * 2
    whole = lambda shape: pl.BlockSpec(shape, lambda *_: (0,) * len(shape))
    table_spec = pl.BlockSpec((degrees // 2, 2, GROUP, half_cycles), lambda g, o: (0, 0, g, 0))
    sign_spec = pl.BlockSpec((GROUP, half_cycles), lambda g, o: (g, 0))
    payload_spec = pl.BlockSpec((groups, 2, GROUP, lanes), lambda g, o: (0, 0, g, 0))
    payload = jax.ShapeDtypeStruct((groups, 2, slots, lanes), bf16)
    table_bytes = degrees * slots * half_cycles * 2
    legendre_cost = pl.CostEstimate(
        flops=1000 * table_bytes, bytes_accessed=table_bytes, transcendentals=0
    )
    tiled = lambda width, height: pltpu.VMEM((width // LANES, height, LANES), f32)
    degree_tiles = tiled(degrees, rows * GROUP)
    cycle_tiles = tiled(half_cycles, rows * GROUP)
    wide = tiled(half_cycles, degrees * GROUP)

    def chunk_spec(q):
        return pl.BlockSpec((CHUNK, 2, GROUP, degrees), lambda g, o: (q, 0, g, 0))

    def synth(q):
        return pl.pallas_call(
            synth_kernel,
            name="synth",
            grid_spec=pltpu.PrefetchScalarGridSpec(
                num_scalar_prefetch=1,
                grid=(slots // GROUP,),
                in_specs=[chunk_spec(q), whole(root.shape), table_spec, sign_spec],
                out_specs=payload_spec,
                scratch_shapes=[
                    degree_tiles,
                    wide,
                    pltpu.VMEM((GROUP, 2 * rows, half_cycles), f32),
                    cycle_tiles,
                    cycle_tiles,
                ],
            ),
            out_shape=payload,
            compiler_params=params(),
            cost_estimate=legendre_cost,
        )(my_orders, probes_in, root, table, sign)

    def analyse(q, returned, held):
        first = held is None
        return pl.pallas_call(
            analysis_kernel,
            name="analyse",
            grid_spec=pltpu.PrefetchScalarGridSpec(
                num_scalar_prefetch=1,
                grid=(slots // GROUP,),
                in_specs=[payload_spec, whole(root.shape), table_spec, sign_spec]
                + ([] if first else [pl.BlockSpec(memory_space=pl.ANY)]),
                out_specs=chunk_spec(q),
                scratch_shapes=[
                    cycle_tiles,
                    cycle_tiles,
                    wide,
                    pltpu.VMEM((GROUP, 4 * rows, half_cycles), bf16),
                    degree_tiles,
                ],
            ),
            out_shape=jax.ShapeDtypeStruct((probes, 2, slots, degrees), f32),
            input_output_aliases={} if first else {5: 0},
            compiler_params=params(),
            cost_estimate=legendre_cost,
        )(my_orders, returned, root, table, sign, *([] if first else [held]))

    ahead_spec = pl.BlockSpec((1, 2 * TILE, orders_count), lambda i, h: (i, 0, 0))
    back_spec = pl.BlockSpec((2 * orders_count, TILE), lambda i, h: (0, i))
    grid_spec = pl.BlockSpec((TILE, part_lanes), lambda i, h: (i, 0))

    def fourier(received, tables, w_low, w_high, turn, chunk_beta, old):
        first = old is None
        ahead, back = tables
        square = jax.ShapeDtypeStruct((half_lon, part_lanes), f32)
        return pl.pallas_call(
            functools.partial(fourier_kernel, first=first),
            name="fourier",
            grid=(half_lon // TILE, parts),
            in_specs=[whole(payload.shape)]
            + [ahead_spec] * 2
            + [back_spec] * 2
            + [grid_spec] * 2
            + [whole((orders_count, 1)), whole((1, lanes))]
            + ([] if first else [grid_spec] * 2),
            out_specs=[whole(payload.shape), grid_spec, grid_spec],
            out_shape=[payload, square, square],
            scratch_shapes=[pltpu.VMEM((parts, orders_count, part_lanes), bf16)] * 2
            + [pltpu.VMEM((parts, orders_count, part_lanes), f32)] * 2
            + [pltpu.VMEM((parts, 1, part_lanes), f32)],
            input_output_aliases={} if first else {9: 1, 10: 2},
            compiler_params=params(),
            cost_estimate=pl.CostEstimate(
                flops=40 * half_lon * lanes * orders_count,
                bytes_accessed=16 * half_lon * orders_count + 16 * half_lon * part_lanes,
                transcendentals=0,
            ),
        )(received, *ahead, *back, w_low, w_high, turn, chunk_beta, *([] if first else old))

    def exchange(x):
        return lax.all_to_all(x, axes, split_axis=0, concat_axis=0, tiled=True)

    local = jnp.arange(cycles, dtype=jnp.int32)
    flipped = jnp.where(south, cycles - 1 - local, local)
    cycle_index = (my_index * cycles + flipped).astype(f32)
    area = 2.0 * math.pi / lon_count * (math.pi / all_cycles) * jnp.sin(
        math.pi * (cycle_index + 0.5) / all_cycles
    )
    turned = jnp.where(south, jnp.flip(weight, 0), weight)
    turned = (area[:, None] * turned).T
    w_low = jnp.tile(turned[:half_lon], (1, PART))
    w_high = jnp.concatenate(
        [turned[half_lon : half_lon + 1], jnp.flip(turned[half_lon + 1 :], 0)], axis=0
    )
    w_high = jnp.tile(w_high, (1, PART))
    turn = (1 - 2 * (order_slots % 2)).astype(f32)[:, None]
    tables = half_tables(order_slots, lon_count)

    received = [exchange(synth(q)) for q in range(chunks)]
    old, held = None, None
    returned = []
    for q in range(chunks):
        chunk_beta = jnp.repeat(beta[q * CHUNK : (q + 1) * CHUNK], cycles)[None, :]
        analysed, low, high = fourier(received[q], tables, w_low, w_high, turn, chunk_beta, old)
        old = (low, high)
        returned.append(exchange(analysed))
    for q in range(chunks):
        held = analyse(q, returned[q], held)

    lane_cycle = jnp.arange(part_lanes, dtype=jnp.int32) % cycles
    pick = (lane_cycle[None, :] == flipped[:, None]).astype(f32)
    sums = [
        lax.dot_general(
            pick, s, (((1,), (1,)), ((), ())), precision=lax.Precision.HIGHEST,
            preferred_element_type=f32,
        )
        for s in old
    ]
    natural = 2.0 * math.pi / lon_count * (math.pi / all_cycles) * jnp.sin(
        math.pi * ((my_index * cycles + local).astype(f32) + 0.5) / all_cycles
    )
    terms = jnp.concatenate([sums[0], sums[1][:, :1], jnp.flip(sums[1][:, 1:], 1)], axis=1)
    gradient = lax.psum_scatter(
        terms * natural[:, None], "probe", scatter_dimension=1, tiled=True
    )
    return (held, gradient)


def body(probes_in, root_spectrum, order_slots, legendre, weight, beta):
    degrees, slots, all_cycles = legendre.shape
    fits = (
        slots % GROUP == 0
        and degrees % DEPTH == 0
        and degrees == order_slots.shape[0]
        and all_cycles % (2 * LANES) == 0
        and (PART * weight.shape[0]) % LANES == 0
        and probes_in.shape[0] % CHUNK == 0
        and weight.shape[1] % (2 * TILE) == 0
        and lax.axis_size(("lat", "blk")) % 2 == 0
    )
    chosen = fast_body if fits else plain_body
    return chosen(probes_in, root_spectrum, order_slots, legendre, weight, beta)


def solution(mesh):
    return jax.shard_map(
        body,
        mesh=mesh,
        in_specs=(
            P("probe", None, ("lat", "blk"), None),
            P(),
            P(),
            P(None, ("lat", "blk"), None),
            P(("lat", "blk"), None),
            P("probe"),
        ),
        out_specs=(P("probe", None, ("lat", "blk"), None), P(("lat", "blk"), "probe")),
        check_vma=False,
    )
```

profile of v0, /device:TPU:0, one launch (start us, length us, event | category | flops | bytes accessed | tf_op | source)
XLA Modules:
  0.0 395.4 jit_solution(4534468561073835415)
XLA Ops:
  10.5 29.0 %synth.3 = bf16[16,2,40,1280]{3,2,1,0:T(8,128)(2,1)} custom-call(s32[40]{0:T(128)} %get-tuple-element.31.orders_ref.refs_0_, bf16[32,2,40,640]{3,2,1,0:T(8,128)(2,1)} %x_ref.3, f32[1,640]{1,0:T(1,128)} %broadcast_in_dim.10.root_ref.refs_2_, bf16[320,2,40,1280]{3,2,1,0:T(8,128)(2,1)} %bitcast.40, f32[40,640]{1,0:T(8,128)} %broadcast_in_dim.11.sign_ref.refs_4_), custom_call_target="tpu_custom_call" | custom-call | flops 32768000000 | bytes 32768000 | tf_op jit(solution)/shard_map/synth/pallas_call | solution.py:355
  39.5 7.6 %all-to-all-start.1 = ((bf16[16,2,40,1280]{3,2,1,0:T(8,128)(2,1)}), bf16[16,2,40,1280]{3,2,1,0:T(8,128)(2,1)}, u32[]{:S(2)}, u32[]{:S(2)}) async-start(bf16[16,2,40,1280]{3,2,1,0:T(8,128)(2,1)} %synth.3), calls=%async_computation.1 | async-start | bytes 6553600 | tf_op jit(solution)/shard_map/all_to_all | solution.py:434
  50.2 1.3 fusion.6
  51.8 2.6 multiply_add_fusion
  54.4 4.5 %copy.19 = f32[640,1280]{1,0:T(8,128)} copy(f32[640,1280]{0,1:T(8,128)} %bitcast.31) | data formatting | bytes 6553600 | tf_op jit(solution)/shard_map/add | solution.py:289
  58.9 3.0 copy.17
  61.9 4.4 %reverse = f32[1280,80]{0,1:T(8,128)S(1)} reverse(f32[1280,80]{0,1:T(8,128)} %bitcast.36), dimensions={0} | reverse | bytes 819200
  66.9 3.2 copy.25.refs_6_
  71.3 3.2 copy.24.refs_5_
  76.2 1.9 multiply_add_fusion.1
  79.2 2.0 pad_maximum_fusion.1.refs_2_
  81.2 2.1 pad_maximum_fusion.refs_1_
  83.3 28.7 %synth.2 = bf16[16,2,40,1280]{3,2,1,0:T(8,128)(2,1)} custom-call(s32[40]{0:T(128)} %get-tuple-element.31.orders_ref.refs_0_, bf16[32,2,40,640]{3,2,1,0:T(8,128)(2,1)} %x_ref.3, f32[1,640]{1,0:T(1,128)} %broadcast_in_dim.10.root_ref.refs_2_, bf16[320,2,40,1280]{3,2,1,0:T(8,128)(2,1)} %bitcast.41, f32[40,640]{1,0:T(8,128)} %broadcast_in_dim.11.sign_ref.refs_4_), custom_call_target="tpu_custom_call" | custom-call | flops 32768000000 | bytes 32768000 | tf_op jit(solution)/shard_map/synth/pallas_call | solution.py:355
  112.0 9.7 %all-to-all-done.1.refs_0_ = bf16[16,2,40,1280]{3,2,1,0:T(8,128)(2,1)} async-done(((bf16[16,2,40,1280]{3,2,1,0:T(8,128)(2,1)}), bf16[16,2,40,1280]{3,2,1,0:T(8,128)(2,1)}, u32[]{:S(2)}, u32[]{:S(2)}) %all-to-all-start.1) | async-done | bytes 3276832 | tf_op jit(solution)/shard_map/all_to_all | solution.py:434
  121.7 4.7 %all-to-all-start = ((bf16[16,2,40,1280]{3,2,1,0:T(8,128)(2,1)}), bf16[16,2,40,1280]{3,2,1,0:T(8,128)(2,1)}, u32[]{:S(2)}, u32[]{:S(2)}) async-start(bf16[16,2,40,1280]{3,2,1,0:T(8,128)(2,1)} %synth.2), calls=%async_computation | async-start | bytes 6553600 | tf_op jit(solution)/shard_map/all_to_all | solution.py:434
  126.8 1.6 copy-done
  128.7 3.1 pad_maximum_fusion.2
  131.8 40.3 %fourier.2 = (bf16[16,2,40,1280]{3,2,1,0:T(8,128)(2,1)}, f32[1280,640]{1,0:T(8,128)}, f32[1280,640]{1,0:T(8,128)}) custom-call(bf16[16,2,40,1280]{3,2,1,0:T(8,128)(2,1)} %all-to-all-done.1.refs_0_, bf16[5,512,640]{2,1,0:T(8,128)(2,1)} %pad_maximum_fusion.refs_1_, bf16[5,512,640]{2,1,0:T(8,128)(2,1)} %pad_maximum_fusion.1.refs_2_, ...), custom_call_target="tpu_custom_call" | custom-call | flops 41943040000 | bytes 26214400 | tf_op jit(solution)/shard_map/fourier/pallas_call | solution.py:409
  172.1 28.7 %all-to-all-done.refs_0_ = bf16[16,2,40,1280]{3,2,1,0:T(8,128)(2,1)} async-done(((bf16[16,2,40,1280]{3,2,1,0:T(8,128)(2,1)}), bf16[16,2,40,1280]{3,2,1,0:T(8,128)(2,1)}, u32[]{:S(2)}, u32[]{:S(2)}) %all-to-all-start) | async-done | bytes 3276832 | tf_op jit(solution)/shard_map/all_to_all | solution.py:434
  200.8 3.7 all-to-all-start.3
  205.4 41.1 %fourier.3 = (bf16[16,2,40,1280]{3,2,1,0:T(8,128)(2,1)}, f32[1280,640]{1,0:T(8,128)}, f32[1280,640]{1,0:T(8,128)}) custom-call(bf16[16,2,40,1280]{3,2,1,0:T(8,128)(2,1)} %all-to-all-done.refs_0_, bf16[5,512,640]{2,1,0:T(8,128)(2,1)} %pad_maximum_fusion.refs_1_, ...), custom_call_target="tpu_custom_call", output_to_operand_aliasing={{1}: (9, {}), {2}: (10, {})} | custom-call | flops 41943040000 | bytes 26214400 | tf_op jit(solution)/shard_map/fourier/pallas_call | solution.py:409
  246.4 32.7 %all-to-all-done.3.refs_1_ = bf16[16,2,40,1280]{3,2,1,0:T(8,128)(2,1)S(1)} async-done(((bf16[16,2,40,1280]{3,2,1,0:T(8,128)(2,1)}), bf16[16,2,40,1280]{3,2,1,0:T(8,128)(2,1)S(1)}, u32[]{:S(2)}, u32[]{:S(2)}) %all-to-all-start.3) | async-done | bytes 3276832 | tf_op jit(solution)/shard_map/all_to_all | solution.py:434
  279.2 1.8 copy-done.3
  280.9 4.5 %all-to-all-start.2 = ((bf16[16,2,40,1280]{3,2,1,0:T(8,128)(2,1)}), bf16[16,2,40,1280]{3,2,1,0:T(8,128)(2,1)}, u32[]{:S(2)}, u32[]{:S(2)}) async-start(bf16[16,2,40,1280]{3,2,1,0:T(8,128)(2,1)} %get-tuple-element.18), calls=%async_computation.2 | async-start | bytes 6553600 | tf_op jit(solution)/shard_map/all_to_all | solution.py:434
  285.8 3.8 fusion.9
  290.5 6.0 %reverse.1 = f32[80,1280]{1,0:T(8,128)} reverse(f32[80,1280]{1,0:T(8,128)} %bitcast.37), dimensions={1} | reverse | bytes 819200
  296.5 2.0 slice.34
  298.4 2.5 fusion.11
  300.9 1.4 concatenate.23
  303.3 28.4 %analyse.2.refs_5_ = f32[32,2,40,640]{3,2,1,0:T(8,128)} custom-call(s32[40]{0:T(128)} %get-tuple-element.31.orders_ref.refs_0_, bf16[16,2,40,1280]{3,2,1,0:T(8,128)(2,1)} %copy-done.3, f32[1,640]{1,0:T(1,128)} %broadcast_in_dim.10.root_ref.refs_2_, bf16[320,2,40,1280]{3,2,1,0:T(8,128)(2,1)} %bitcast.42, f32[40,640]{1,0:T(8,128)} %broadcast_in_dim.11.sign_ref.refs_4_), custom_call_target="tpu_custom_call" | custom-call | flops 32768000000 | bytes 32768000 | tf_op jit(solution)/shard_map/analyse/pallas_call | solution.py:378
  331.7 28.3 %all-to-all-done.2.refs_1_ = bf16[16,2,40,1280]{3,2,1,0:T(8,128)(2,1)} async-done(((bf16[16,2,40,1280]{3,2,1,0:T(8,128)(2,1)}), bf16[16,2,40,1280]{3,2,1,0:T(8,128)(2,1)}, u32[]{:S(2)}, u32[]{:S(2)}) %all-to-all-start.2) | async-done | bytes 3276832 | tf_op jit(solution)/shard_map/all_to_all | solution.py:434
  360.1 28.4 %analyse.3 = f32[32,2,40,640]{3,2,1,0:T(8,128)} custom-call(s32[40]{0:T(128)} %get-tuple-element.31.orders_ref.refs_0_, bf16[16,2,40,1280]{3,2,1,0:T(8,128)(2,1)} %all-to-all-done.2.refs_1_, f32[1,640]{1,0:T(1,128)} %broadcast_in_dim.10.root_ref.refs_2_, bf16[320,2,40,1280]{3,2,1,0:T(8,128)(2,1)} %bitcast.43, ...), custom_call_target="tpu_custom_call", output_to_operand_aliasing={{}: (5, {})} | custom-call | flops 32768000000 | bytes 32768000 | tf_op jit(solution)/shard_map/analyse/pallas_call | solution.py:378
  (57 shorter events, 15.0 us)
Async XLA Ops:
  39.5 7.6 %copy-start.5 = (f32[80,2560]{1,0:T(8,128)S(1)}, f32[80,2560]{1,0:T(8,128)}, u32[]{:S(2)}) copy-start(f32[80,2560]{1,0:T(8,128)} %param.10) | copy-start | bytes 2457604
  39.5 82.2 %all-to-all-start.1 = ((bf16[16,2,40,1280]{3,2,1,0:T(8,128)(2,1)}), bf16[16,2,40,1280]{3,2,1,0:T(8,128)(2,1)}, u32[]{:S(2)}, u32[]{:S(2)}) async-start(bf16[16,2,40,1280]{3,2,1,0:T(8,128)(2,1)} %synth.3), calls=%async_computation.1 | async-start | bytes 6553600 | tf_op jit(solution)/shard_map/all_to_all | solution.py:434
  47.1 3.1 copy-start.9
  48.3 3.4 copy-start.2
  51.5 2.9 copy-start.6
  51.5 2.9 copy-start.7
  58.9 7.5 %slice-start = ((f32[2560,80]{0,1:T(8,128)}), f32[1,80]{0,1:T(8,128)S(1)}, s32[]{:S(2)}) async-start(f32[2560,80]{0,1:T(8,128)} %copy-done.2), calls=%async_computation.6 | async-start | bytes 81920 | tf_op jit(solution)/shard_map/slice | solution.py:446
  71.3 4.1 %copy-start.11 = (f32[32]{0:T(128)S(1)}, f32[32]{0:T(128)}, u32[]{:S(2)}) copy-start(f32[32]{0:T(128)} %param.11) | copy-start | bytes 388
  112.0 14.4 %copy-start.1 = (f32[640,1280]{1,0:T(8,128)S(1)}, f32[640,1280]{1,0:T(8,128)}, u32[]{:S(2)}) copy-start(f32[640,1280]{1,0:T(8,128)} %copy.19) | copy-start | bytes 9830404
  121.7 79.1 %all-to-all-start = ((bf16[16,2,40,1280]{3,2,1,0:T(8,128)(2,1)}), bf16[16,2,40,1280]{3,2,1,0:T(8,128)(2,1)}, u32[]{:S(2)}, u32[]{:S(2)}) async-start(bf16[16,2,40,1280]{3,2,1,0:T(8,128)(2,1)} %synth.2), calls=%async_computation | async-start | bytes 6553600 | tf_op jit(solution)/shard_map/all_to_all | solution.py:434
  126.4 1.9 copy-start
  200.8 78.3 %all-to-all-start.3 = ((bf16[16,2,40,1280]{3,2,1,0:T(8,128)(2,1)}), bf16[16,2,40,1280]{3,2,1,0:T(8,128)(2,1)S(1)}, u32[]{:S(2)}, u32[]{:S(2)}) async-start(bf16[16,2,40,1280]{3,2,1,0:T(8,128)(2,1)} %get-tuple-element.19), calls=%async_computation.3 | async-start | bytes 6553600 | tf_op jit(solution)/shard_map/all_to_all | solution.py:434
  279.2 1.8 copy-start.3
  280.9 79.1 %all-to-all-start.2 = ((bf16[16,2,40,1280]{3,2,1,0:T(8,128)(2,1)}), bf16[16,2,40,1280]{3,2,1,0:T(8,128)(2,1)}, u32[]{:S(2)}, u32[]{:S(2)}) async-start(bf16[16,2,40,1280]{3,2,1,0:T(8,128)(2,1)} %get-tuple-element.18), calls=%async_computation.2 | async-start | bytes 6553600 | tf_op jit(solution)/shard_map/all_to_all | solution.py:434
  285.5 13.0 %copy-start.4 = (f32[1280,640]{1,0:T(8,128)S(1)}, f32[1280,640]{1,0:T(8,128)}, u32[]{:S(2)}) copy-start(f32[1280,640]{1,0:T(8,128)} %get-tuple-element.20) | copy-start | bytes 9830404
  285.5 103.0 %reduce-scatter.2.cloned.1.call-start = ((), (), s32[]{:S(2)}) async-start(), calls=%async_computation.5 | async-start | bytes 1228800 | tf_op jit(solution)/shard_map/reduce_scatter | solution.py:476
  289.5 0.9 copy-start.8
  290.5 10.4 %slice-start.1 = ((f32[80,1280]{1,0:T(8,128)}), f32[80,1]{1,0:T(8,128)S(1)}, s32[]{:S(2)}) async-start(f32[80,1280]{1,0:T(8,128)} %copy-done.8), calls=%async_computation.7 | async-start | bytes 81920 | tf_op jit(solution)/shard_map/slice | solution.py:475
  296.5 5.8 %copy-start.10 = (f32[80]{0:T(128)S(1)}, f32[80]{0:T(128)}, u32[]{:S(2)}) copy-start(f32[80]{0:T(128)} %get-tuple-element.44) | copy-start | bytes 964
Sparse Core Ops, SparseCore 0:
  303.4 19.0 reduce-scatter.1
where the time goes:
time: 397 us; the launch traced here: 395 us
  Pallas kernels  196 us (49%)
  waiting for transfers between devices  99.5 us (25%)
  local copies, waits for them, and re-layouts  40.3 us (10%)
  starting transfers between devices  20.8 us (5%)
  other arithmetic  18.3 us (5%)
  between operations  14.3 us (4%)
  matrix products  6.25 us (2%)
    all_to_all x4, waiting for transfers between devices, exchange(): return lax.all_to_all(x, axes, split_axis=0, concat_axis=0, tiled=True)  99.5 us
    pallas_call x2, Pallas kernels, fourier(): pl.pallas_call(functools.partial(fourier_kernel, first=first), name='four...  81.4 us
    pallas_call x2, Pallas kernels, synth(): pl.pallas_call(synth_kernel, name='synth', grid_spec=pltpu.PrefetchScalar...  57.7 us
    pallas_call x2, Pallas kernels, analyse(): pl.pallas_call(analysis_kernel, name='analyse', grid_spec=pltpu.PrefetchS...  56.8 us
    all_to_all x4, starting transfers between devices, exchange(): return lax.all_to_all(x, axes, split_axis=0, concat_axis=0, tiled=True)  20.5 us
    unnamed x28, local copies, waits for them, and re-layouts  15.8 us
  transfers between devices with their start and end apart: 5, of which 4 were waited for; matrix products, arithmetic and copies ran while one was open for 15% of the time, Pallas kernels for 42%

commit v1 on v0

--- a/solution.py
+++ b/solution.py
@@ -472,10 +472,18 @@
     natural = 2.0 * math.pi / lon_count * (math.pi / all_cycles) * jnp.sin(
         math.pi * ((my_index * cycles + local).astype(f32) + 0.5) / all_cycles
     )
-    terms = jnp.concatenate([sums[0], sums[1][:, :1], jnp.flip(sums[1][:, 1:], 1)], axis=1)
-    gradient = lax.psum_scatter(
-        terms * natural[:, None], "probe", scatter_dimension=1, tiled=True
-    )
+    if lax.axis_size("probe") == 2:
+        ahead_half = lax.axis_index("probe") == 0
+        keep = jnp.where(ahead_half, sums[0], sums[1])
+        give = jnp.where(ahead_half, sums[1], sums[0])
+        half = (keep + lax.ppermute(give, "probe", [(0, 1), (1, 0)])) * natural[:, None]
+        mirrored = jnp.concatenate([half[:, :1], jnp.flip(half[:, 1:], 1)], axis=1)
+        gradient = jnp.where(ahead_half, half, mirrored)
+    else:
+        terms = jnp.concatenate([sums[0], sums[1][:, :1], jnp.flip(sums[1][:, 1:], 1)], axis=1)
+        gradient = lax.psum_scatter(
+            terms * natural[:, None], "probe", scatter_dimension=1, tiled=True
+        )
     return (held, gradient)
 
 

time: 397 us -> 383 us (0.965)
  between operations: 14.3 us -> 0.93 us
  local copies, waits for them, and re-layouts: 40.3 us -> 31.1 us
  waiting for transfers between devices: 99.5 us -> 108 us
    ppermute x0 -> x1, waiting for transfers between devices: none -> 9.87 us  [fast_body(): lax.ppermute(give, 'probe', [(0, 1), (1, 0)])]
    unnamed x28 -> x24, local copies, waits for them, and re-layouts: 15.8 us -> 8.88 us
  transfers between devices with their start and end apart: 5 -> 5, of which waited for: 4 -> 5; matrix products, arithmetic and copies ran while one was open for 15% -> 13% of each run, Pallas kernels for 42% -> 36%
where the time goes in v1:
time: 383 us; the launch traced here: 382 us
  Pallas kernels  196 us (51%)
  waiting for transfers between devices  108 us (28%)
  local copies, waits for them, and re-layouts  31.1 us (8%)
  starting transfers between devices  22.3 us (6%)
  other arithmetic  17.9 us (5%)
  matrix products  5.53 us (1%)
    all_to_all x4, waiting for transfers between devices, exchange(): return lax.all_to_all(x, axes, split_axis=0, concat_axis=0, tiled=True)  98.5 us
    pallas_call x2, Pallas kernels, fourier(): pl.pallas_call(functools.partial(fourier_kernel, first=first), name='four...  81.4 us
    pallas_call x2, Pallas kernels, synth(): pl.pallas_call(synth_kernel, name='synth', grid_spec=pltpu.PrefetchScalar...  57.6 us
    pallas_call x2, Pallas kernels, analyse(): pl.pallas_call(analysis_kernel, name='analyse', grid_spec=pltpu.PrefetchS...  56.6 us
    all_to_all x4, starting transfers between devices, exchange(): return lax.all_to_all(x, axes, split_axis=0, concat_axis=0, tiled=True)  20.7 us
    ppermute x1, waiting for transfers between devices, fast_body(): lax.ppermute(give, 'probe', [(0, 1), (1, 0)])  9.87 us
    unnamed x24, local copies, waits for them, and re-layouts  8.88 us
  transfers between devices with their start and end apart: 5, of which 5 were waited for; matrix products, arithmetic and copies ran while one was open for 13% of the time, Pallas kernels for 36%

profile of v1, /device:TPU:0, one launch (start us, length us, event | category | flops | bytes accessed | tf_op | source)
XLA Modules:
  0.0 381.7 jit_solution(1633744900809018291)
XLA Ops:
  1.9 1.3 fusion.33
  3.9 28.9 %synth.3 = bf16[16,2,40,1280]{3,2,1,0:T(8,128)(2,1)} custom-call(s32[40]{0:T(128)} %get-tuple-element.31.orders_ref.refs_0_, bf16[32,2,40,640]{3,2,1,0:T(8,128)(2,1)} %x_ref.3, f32[1,640]{1,0:T(1,128)} %broadcast_in_dim.10.root_ref.refs_2_, bf16[320,2,40,1280]{3,2,1,0:T(8,128)(2,1)} %bitcast.40, f32[40,640]{1,0:T(8,128)} %broadcast_in_dim.11.sign_ref.refs_4_), custom_call_target="tpu_custom_call" | custom-call | flops 32768000000 | bytes 32768000 | tf_op jit(solution)/shard_map/synth/pallas_call | solution.py:355
  32.8 7.6 %all-to-all-start.1 = ((bf16[16,2,40,1280]{3,2,1,0:T(8,128)(2,1)}), bf16[16,2,40,1280]{3,2,1,0:T(8,128)(2,1)}, u32[]{:S(2)}, u32[]{:S(2)}) async-start(bf16[16,2,40,1280]{3,2,1,0:T(8,128)(2,1)} %synth.3), calls=%async_computation.1 | async-start | bytes 6553600 | tf_op jit(solution)/shard_map/all_to_all | solution.py:434
  43.0 1.3 fusion.6
  44.6 2.6 multiply_add_fusion
  47.2 4.6 %copy.19 = f32[640,1280]{1,0:T(8,128)} copy(f32[640,1280]{0,1:T(8,128)} %bitcast.31) | data formatting | bytes 6553600 | tf_op jit(solution)/shard_map/add | solution.py:289
  51.7 3.0 copy.17
  54.7 4.4 %reverse = f32[1280,80]{0,1:T(8,128)S(1)} reverse(f32[1280,80]{0,1:T(8,128)} %bitcast.36), dimensions={0} | reverse | bytes 819200
  59.7 3.1 copy.25.refs_6_
  64.1 3.2 copy.24.refs_5_
  69.0 1.9 multiply_add_fusion.1
  72.1 2.0 pad_maximum_fusion.1.refs_2_
  74.0 2.1 pad_maximum_fusion.refs_1_
  76.1 28.6 %synth.2 = bf16[16,2,40,1280]{3,2,1,0:T(8,128)(2,1)} custom-call(s32[40]{0:T(128)} %get-tuple-element.31.orders_ref.refs_0_, bf16[32,2,40,640]{3,2,1,0:T(8,128)(2,1)} %x_ref.3, f32[1,640]{1,0:T(1,128)} %broadcast_in_dim.10.root_ref.refs_2_, bf16[320,2,40,1280]{3,2,1,0:T(8,128)(2,1)} %bitcast.41, f32[40,640]{1,0:T(8,128)} %broadcast_in_dim.11.sign_ref.refs_4_), custom_call_target="tpu_custom_call" | custom-call | flops 32768000000 | bytes 32768000 | tf_op jit(solution)/shard_map/synth/pallas_call | solution.py:355
  104.8 10.3 %all-to-all-done.1.refs_0_ = bf16[16,2,40,1280]{3,2,1,0:T(8,128)(2,1)} async-done(((bf16[16,2,40,1280]{3,2,1,0:T(8,128)(2,1)}), bf16[16,2,40,1280]{3,2,1,0:T(8,128)(2,1)}, u32[]{:S(2)}, u32[]{:S(2)}) %all-to-all-start.1) | async-done | bytes 3276832 | tf_op jit(solution)/shard_map/all_to_all | solution.py:434
  115.1 4.7 %all-to-all-start = ((bf16[16,2,40,1280]{3,2,1,0:T(8,128)(2,1)}), bf16[16,2,40,1280]{3,2,1,0:T(8,128)(2,1)}, u32[]{:S(2)}, u32[]{:S(2)}) async-start(bf16[16,2,40,1280]{3,2,1,0:T(8,128)(2,1)} %synth.2), calls=%async_computation | async-start | bytes 6553600 | tf_op jit(solution)/shard_map/all_to_all | solution.py:434
  120.1 1.6 copy-done
  122.0 3.2 pad_maximum_fusion.2
  125.2 40.3 %fourier.2 = (bf16[16,2,40,1280]{3,2,1,0:T(8,128)(2,1)}, f32[1280,640]{1,0:T(8,128)}, f32[1280,640]{1,0:T(8,128)}) custom-call(bf16[16,2,40,1280]{3,2,1,0:T(8,128)(2,1)} %all-to-all-done.1.refs_0_, bf16[5,512,640]{2,1,0:T(8,128)(2,1)} %pad_maximum_fusion.refs_1_, bf16[5,512,640]{2,1,0:T(8,128)(2,1)} %pad_maximum_fusion.1.refs_2_, ...), custom_call_target="tpu_custom_call" | custom-call | flops 41943040000 | bytes 26214400 | tf_op jit(solution)/shard_map/fourier/pallas_call | solution.py:409
  165.5 28.7 %all-to-all-done.refs_0_ = bf16[16,2,40,1280]{3,2,1,0:T(8,128)(2,1)} async-done(((bf16[16,2,40,1280]{3,2,1,0:T(8,128)(2,1)}), bf16[16,2,40,1280]{3,2,1,0:T(8,128)(2,1)}, u32[]{:S(2)}, u32[]{:S(2)}) %all-to-all-start) | async-done | bytes 3276832 | tf_op jit(solution)/shard_map/all_to_all | solution.py:434
  194.2 3.7 all-to-all-start.3
  198.7 41.1 %fourier.3 = (bf16[16,2,40,1280]{3,2,1,0:T(8,128)(2,1)}, f32[1280,640]{1,0:T(8,128)}, f32[1280,640]{1,0:T(8,128)}) custom-call(bf16[16,2,40,1280]{3,2,1,0:T(8,128)(2,1)} %all-to-all-done.refs_0_, bf16[5,512,640]{2,1,0:T(8,128)(2,1)} %pad_maximum_fusion.refs_1_, ...), custom_call_target="tpu_custom_call", output_to_operand_aliasing={{1}: (9, {}), {2}: (10, {})} | custom-call | flops 41943040000 | bytes 26214400 | tf_op jit(solution)/shard_map/fourier/pallas_call | solution.py:409
  239.8 32.8 %all-to-all-done.3.refs_1_ = bf16[16,2,40,1280]{3,2,1,0:T(8,128)(2,1)S(1)} async-done(((bf16[16,2,40,1280]{3,2,1,0:T(8,128)(2,1)}), bf16[16,2,40,1280]{3,2,1,0:T(8,128)(2,1)S(1)}, u32[]{:S(2)}, u32[]{:S(2)}) %all-to-all-start.3) | async-done | bytes 3276832 | tf_op jit(solution)/shard_map/all_to_all | solution.py:434
  272.5 1.7 copy-done.3
  274.3 4.7 %all-to-all-start.2 = ((bf16[16,2,40,1280]{3,2,1,0:T(8,128)(2,1)}), bf16[16,2,40,1280]{3,2,1,0:T(8,128)(2,1)}, u32[]{:S(2)}, u32[]{:S(2)}) async-start(bf16[16,2,40,1280]{3,2,1,0:T(8,128)(2,1)} %get-tuple-element.18), calls=%async_computation.2 | async-start | bytes 6553600 | tf_op jit(solution)/shard_map/all_to_all | solution.py:434
  279.0 3.8 fusion.11
  282.8 1.7 broadcast_select_fusion
  284.6 1.6 collective-permute-start
  286.2 9.9 %collective-permute-done = f32[80,1280]{1,0:T(8,128)S(1)} collective-permute-done((f32[80,1280]{1,0:T(8,128)S(1)}, f32[80,1280]{1,0:T(8,128)S(1)}, u32[]{:S(2)}, u32[]{:S(2)}) %collective-permute-start) | collective-permute-done | bytes 409632 | tf_op jit(solution)/shard_map/ppermute | solution.py:479
  298.3 28.3 %analyse.2.refs_5_ = f32[32,2,40,640]{3,2,1,0:T(8,128)} custom-call(s32[40]{0:T(128)} %get-tuple-element.31.orders_ref.refs_0_, bf16[16,2,40,1280]{3,2,1,0:T(8,128)(2,1)} %copy-done.3, f32[1,640]{1,0:T(1,128)} %broadcast_in_dim.10.root_ref.refs_2_, bf16[320,2,40,1280]{3,2,1,0:T(8,128)(2,1)} %bitcast.42, f32[40,640]{1,0:T(8,128)} %broadcast_in_dim.11.sign_ref.refs_4_), custom_call_target="tpu_custom_call" | custom-call | flops 32768000000 | bytes 32768000 | tf_op jit(solution)/shard_map/analyse/pallas_call | solution.py:378
  326.6 26.8 %all-to-all-done.2.refs_1_ = bf16[16,2,40,1280]{3,2,1,0:T(8,128)(2,1)} async-done(((bf16[16,2,40,1280]{3,2,1,0:T(8,128)(2,1)}), bf16[16,2,40,1280]{3,2,1,0:T(8,128)(2,1)}, u32[]{:S(2)}, u32[]{:S(2)}) %all-to-all-start.2) | async-done | bytes 3276832 | tf_op jit(solution)/shard_map/all_to_all | solution.py:434
  353.4 28.3 %analyse.3 = f32[32,2,40,640]{3,2,1,0:T(8,128)} custom-call(s32[40]{0:T(128)} %get-tuple-element.31.orders_ref.refs_0_, bf16[16,2,40,1280]{3,2,1,0:T(8,128)(2,1)} %all-to-all-done.2.refs_1_, f32[1,640]{1,0:T(1,128)} %broadcast_in_dim.10.root_ref.refs_2_, bf16[320,2,40,1280]{3,2,1,0:T(8,128)(2,1)} %bitcast.43, ...), custom_call_target="tpu_custom_call", output_to_operand_aliasing={{}: (5, {})} | custom-call | flops 32768000000 | bytes 32768000 | tf_op jit(solution)/shard_map/analyse/pallas_call | solution.py:378
  (52 shorter events, 13.2 us)
Async XLA Ops:
  32.8 7.6 %copy-start.4 = (f32[80,2560]{1,0:T(8,128)S(1)}, f32[80,2560]{1,0:T(8,128)}, u32[]{:S(2)}) copy-start(f32[80,2560]{1,0:T(8,128)} %param.10) | copy-start | bytes 2457604
  32.8 82.2 %all-to-all-start.1 = ((bf16[16,2,40,1280]{3,2,1,0:T(8,128)(2,1)}), bf16[16,2,40,1280]{3,2,1,0:T(8,128)(2,1)}, u32[]{:S(2)}, u32[]{:S(2)}) async-start(bf16[16,2,40,1280]{3,2,1,0:T(8,128)(2,1)} %synth.3), calls=%async_computation.1 | async-start | bytes 6553600 | tf_op jit(solution)/shard_map/all_to_all | solution.py:434
  40.4 2.6 copy-start.8
  41.2 3.4 copy-start.2
  44.3 2.9 copy-start.6
  44.3 2.9 copy-start.7
  51.7 7.5 %slice-start = ((f32[2560,80]{0,1:T(8,128)}), f32[1,80]{0,1:T(8,128)S(1)}, s32[]{:S(2)}) async-start(f32[2560,80]{0,1:T(8,128)} %copy-done.2), calls=%async_computation.4 | async-start | bytes 81920 | tf_op jit(solution)/shard_map/slice | solution.py:446
  64.1 4.1 %copy-start.9 = (f32[32]{0:T(128)S(1)}, f32[32]{0:T(128)}, u32[]{:S(2)}) copy-start(f32[32]{0:T(128)} %param.11) | copy-start | bytes 388
  104.8 15.0 %copy-start.1 = (f32[640,1280]{1,0:T(8,128)S(1)}, f32[640,1280]{1,0:T(8,128)}, u32[]{:S(2)}) copy-start(f32[640,1280]{1,0:T(8,128)} %copy.19) | copy-start | bytes 9830404
  115.1 79.1 %all-to-all-start = ((bf16[16,2,40,1280]{3,2,1,0:T(8,128)(2,1)}), bf16[16,2,40,1280]{3,2,1,0:T(8,128)(2,1)}, u32[]{:S(2)}, u32[]{:S(2)}) async-start(bf16[16,2,40,1280]{3,2,1,0:T(8,128)(2,1)} %synth.2), calls=%async_computation | async-start | bytes 6553600 | tf_op jit(solution)/shard_map/all_to_all | solution.py:434
  119.8 1.9 copy-start
  194.2 78.3 %all-to-all-start.3 = ((bf16[16,2,40,1280]{3,2,1,0:T(8,128)(2,1)}), bf16[16,2,40,1280]{3,2,1,0:T(8,128)(2,1)S(1)}, u32[]{:S(2)}, u32[]{:S(2)}) async-start(bf16[16,2,40,1280]{3,2,1,0:T(8,128)(2,1)} %get-tuple-element.19), calls=%async_computation.3 | async-start | bytes 6553600 | tf_op jit(solution)/shard_map/all_to_all | solution.py:434
  272.5 1.7 copy-start.3
  274.3 79.1 %all-to-all-start.2 = ((bf16[16,2,40,1280]{3,2,1,0:T(8,128)(2,1)}), bf16[16,2,40,1280]{3,2,1,0:T(8,128)(2,1)}, u32[]{:S(2)}, u32[]{:S(2)}) async-start(bf16[16,2,40,1280]{3,2,1,0:T(8,128)(2,1)} %get-tuple-element.18), calls=%async_computation.2 | async-start | bytes 6553600 | tf_op jit(solution)/shard_map/all_to_all | solution.py:434
  279.0 3.8 %copy-start.5 = (f32[1280,640]{1,0:T(8,128)S(1)}, f32[1280,640]{1,0:T(8,128)}, u32[]{:S(2)}) copy-start(f32[1280,640]{1,0:T(8,128)} %get-tuple-element.21) | copy-start | bytes 9830404
  284.6 11.5 %collective-permute-start = (f32[80,1280]{1,0:T(8,128)S(1)}, f32[80,1280]{1,0:T(8,128)S(1)}, u32[]{:S(2)}, u32[]{:S(2)}) collective-permute-start(f32[80,1280]{1,0:T(8,128)S(1)} %get-tuple-element.42), channel_id=1, source_target_pairs={{0,1},{1,0},{2,3},{3,2},{4,5},{5,4},{6,7},{7,6},{8,9},{9,8},{10,11... | collective-permute-start | bytes 1228808 | tf_op jit(solution)/shard_map/ppermute | solution.py:479

commit v2 on v1

--- a/solution.py
+++ b/solution.py
@@ -87,10 +87,11 @@
 
 
 LANES = 128
+PITCH = GROUP + 1
 
 
 def every(slot, count):
-    return pl.ds(slot, count, stride=GROUP)
+    return pl.ds(slot, count, stride=PITCH)
 
 
 def tiles(ref):
@@ -112,9 +113,14 @@
         some = pl.ds(step * (DEPTH // 2), DEPTH // 2)
         for t in tiles(wide):
             piece = tbl_ref[some, :, :, t * LANES : (t + 1) * LANES].astype(jnp.float32)
-            wide[t, pl.ds(step * (DEPTH * GROUP), DEPTH * GROUP)] = piece.reshape(
-                DEPTH * GROUP, LANES
-            )
+            piece = piece.reshape(DEPTH, GROUP, LANES)
+            for i in range(DEPTH):
+                wide[t, pl.ds(step * (DEPTH * PITCH) + i * PITCH, GROUP), :] = piece[i]
+
+
+def table_block(wide, step, slot):
+    rows = pl.ds(step * (DEPTH * PITCH) + slot, DEPTH, stride=PITCH)
+    return take(wide, rows).astype(jnp.bfloat16)
 
 
 def visit(orders_ref, group, turn, pair, steps):
@@ -135,7 +141,9 @@
     half = out_ref.shape[0] // 2
     rows = chunk * 2
     scaled = (x_ref[...].astype(jnp.float32) * root_ref[...]).astype(jnp.bfloat16)
-    put(xs, slice(None), scaled.astype(jnp.float32).reshape(rows * GROUP, scaled.shape[-1]))
+    scaled = scaled.astype(jnp.float32).reshape(rows, GROUP, scaled.shape[-1])
+    for i in range(rows):
+        put(xs, pl.ds(i * PITCH, GROUP), scaled[i])
     acc[...] = jnp.zeros_like(acc)
 
     spread_rows(tbl_ref, wide)
@@ -148,7 +156,7 @@
             x = xs[step, every(slot, rows), :]
             even = even_degree(x.shape)
             x = jnp.concatenate([jnp.where(even, x, 0.0), jnp.where(even, 0.0, x)], axis=0)
-            table = take(wide, every(step * (DEPTH * GROUP) + slot, DEPTH)).astype(jnp.bfloat16)
+            table = table_block(wide, step, slot)
             acc[slot] += dot(x.astype(jnp.bfloat16), table)
 
     for slot in range(GROUP):
@@ -158,7 +166,7 @@
     for c in range(2):
         north, south = [], []
         for p in range(chunk):
-            place = pl.ds((2 * p + c) * GROUP, GROUP)
+            place = pl.ds((2 * p + c) * PITCH, GROUP)
             north.append(take(ns, place))
             south.append(take(ss, place) * sign_ref[...])
         for d in range(half):
@@ -183,7 +191,7 @@
             north = jnp.concatenate([blocks[d][:, cut] for d in range(half)], axis=-1)
             other = [blocks[2 * half - 1 - d][:, cut] for d in range(half)]
             south = jnp.concatenate(other, axis=-1) * sign_ref[...]
-            place = pl.ds((2 * p + c) * GROUP, GROUP)
+            place = pl.ds((2 * p + c) * PITCH, GROUP)
             put(plus, place, north + south)
             put(minus, place, north - south)
     for slot in range(GROUP):
@@ -201,16 +209,16 @@
         for pair in range(GROUP // 2):
             slot, step = visit(orders_ref, group, turn, pair, steps)
             now = pl.ds(pl.multiple_of(step * DEPTH, DEPTH), DEPTH)
-            table = take(wide, every(step * (DEPTH * GROUP) + slot, DEPTH)).astype(jnp.bfloat16)
+            table = table_block(wide, step, slot)
             both = dot(held[slot], table, ((1,), (1,)))
             both = both[: 2 * rows] + both[2 * rows :]
             even = even_degree((rows, DEPTH))
             chosen = jnp.where(even, both[:rows], both[rows:])
             outs[step, every(slot, rows), :] = chosen * root_ref[:, now]
 
-    for t in tiles(outs):
-        cut = slice(t * LANES, (t + 1) * LANES)
-        out_ref[:, :, :, cut] = outs[t].reshape(chunk, 2, GROUP, LANES)
+    for p in range(chunk):
+        for c in range(2):
+            out_ref[p, c] = take(outs, pl.ds((2 * p + c) * PITCH, GROUP))
 
 
 def fourier_kernel(*refs, first):
@@ -344,9 +352,9 @@
         flops=1000 * table_bytes, bytes_accessed=table_bytes, transcendentals=0
     )
     tiled = lambda width, height: pltpu.VMEM((width // LANES, height, LANES), f32)
-    degree_tiles = tiled(degrees, rows * GROUP)
-    cycle_tiles = tiled(half_cycles, rows * GROUP)
-    wide = tiled(half_cycles, degrees * GROUP)
+    degree_tiles = tiled(degrees, rows * PITCH)
+    cycle_tiles = tiled(half_cycles, rows * PITCH)
+    wide = tiled(half_cycles, degrees * PITCH)
 
     def chunk_spec(q):
         return pl.BlockSpec((CHUNK, 2, GROUP, degrees), lambda g, o: (q, 0, g, 0))

time: 383 us -> 373 us (0.974)
  Pallas kernels: 196 us -> 176 us
  waiting for transfers between devices: 108 us -> 118 us
    pallas_call x2, Pallas kernels: 57.6 us -> 43.6 us  [synth(): pl.pallas_call(synth_kernel, name='synth', grid_spec=pltpu.PrefetchScalar...]
    all_to_all x4, waiting for transfers between devices: 98.5 us -> 108 us  [exchange(): return lax.all_to_all(x, axes, split_axis=0, concat_axis=0, tiled=True)]
    pallas_call x2, Pallas kernels: 56.6 us -> 51.1 us  [analyse(): pl.pallas_call(analysis_kernel, name='analyse', grid_spec=pltpu.PrefetchS...]
  transfers between devices with their start and end apart: 5 -> 5, of which waited for: 5 -> 5; matrix products, arithmetic and copies ran while one was open for 13% -> 13% of each run, Pallas kernels for 36% -> 35%
where the time goes in v2:
time: 373 us; the launch traced here: 372 us
  Pallas kernels  176 us (47%)
  waiting for transfers between devices  118 us (32%)
  local copies, waits for them, and re-layouts  31.1 us (8%)
  starting transfers between devices  22.3 us (6%)
  other arithmetic  17.9 us (5%)
  matrix products  5.52 us (1%)
    all_to_all x4, waiting for transfers between devices, exchange(): return lax.all_to_all(x, axes, split_axis=0, concat_axis=0, tiled=True)  108 us
    pallas_call x2, Pallas kernels, fourier(): pl.pallas_call(functools.partial(fourier_kernel, first=first), name='four...  81.4 us
    pallas_call x2, Pallas kernels, analyse(): pl.pallas_call(analysis_kernel, name='analyse', grid_spec=pltpu.PrefetchS...  51.1 us
    pallas_call x2, Pallas kernels, synth(): pl.pallas_call(synth_kernel, name='synth', grid_spec=pltpu.PrefetchScalar...  43.6 us
    all_to_all x4, starting transfers between devices, exchange(): return lax.all_to_all(x, axes, split_axis=0, concat_axis=0, tiled=True)  20.7 us
    ppermute x1, waiting for transfers between devices, fast_body(): lax.ppermute(give, 'probe', [(0, 1), (1, 0)])  9.86 us
    unnamed x24, local copies, waits for them, and re-layouts  8.88 us
  transfers between devices with their start and end apart: 5, of which 5 were waited for; matrix products, arithmetic and copies ran while one was open for 13% of the time, Pallas kernels for 35%

profile of v2, /device:TPU:0, one launch (start us, length us, event | category | flops | bytes accessed | tf_op | source)
XLA Modules:
  0.0 371.8 jit_solution(13807244018604479569)
XLA Ops:
  1.9 1.3 fusion.33
  3.9 21.8 %synth.3 = bf16[16,2,40,1280]{3,2,1,0:T(8,128)(2,1)} custom-call(s32[40]{0:T(128)} %get-tuple-element.31.orders_ref.refs_0_, bf16[32,2,40,640]{3,2,1,0:T(8,128)(2,1)} %x_ref.3, f32[1,640]{1,0:T(1,128)} %broadcast_in_dim.10.root_ref.refs_2_, bf16[320,2,40,1280]{3,2,1,0:T(8,128)(2,1)} %bitcast.40, f32[40,640]{1,0:T(8,128)} %broadcast_in_dim.11.sign_ref.refs_4_), custom_call_target="tpu_custom_call" | custom-call | flops 32768000000 | bytes 32768000 | tf_op jit(solution)/shard_map/synth/pallas_call | solution.py:363
  25.7 7.6 %all-to-all-start.1 = ((bf16[16,2,40,1280]{3,2,1,0:T(8,128)(2,1)}), bf16[16,2,40,1280]{3,2,1,0:T(8,128)(2,1)}, u32[]{:S(2)}, u32[]{:S(2)}) async-start(bf16[16,2,40,1280]{3,2,1,0:T(8,128)(2,1)} %synth.3), calls=%async_computation.1 | async-start | bytes 6553600 | tf_op jit(solution)/shard_map/all_to_all | solution.py:442
  35.9 1.3 fusion.6
  37.5 2.6 multiply_add_fusion
  40.1 4.6 %copy.19 = f32[640,1280]{1,0:T(8,128)} copy(f32[640,1280]{0,1:T(8,128)} %bitcast.31) | data formatting | bytes 6553600 | tf_op jit(solution)/shard_map/add | solution.py:297
  44.6 3.0 copy.17
  47.6 4.4 %reverse = f32[1280,80]{0,1:T(8,128)S(1)} reverse(f32[1280,80]{0,1:T(8,128)} %bitcast.36), dimensions={0} | reverse | bytes 819200
  52.6 3.1 copy.25.refs_6_
  57.0 3.2 copy.24.refs_5_
  61.9 1.9 multiply_add_fusion.1
  64.9 2.0 pad_maximum_fusion.1.refs_2_
  66.9 2.1 pad_maximum_fusion.refs_1_
  69.0 21.8 %synth.2 = bf16[16,2,40,1280]{3,2,1,0:T(8,128)(2,1)} custom-call(s32[40]{0:T(128)} %get-tuple-element.31.orders_ref.refs_0_, bf16[32,2,40,640]{3,2,1,0:T(8,128)(2,1)} %x_ref.3, f32[1,640]{1,0:T(1,128)} %broadcast_in_dim.10.root_ref.refs_2_, bf16[320,2,40,1280]{3,2,1,0:T(8,128)(2,1)} %bitcast.41, f32[40,640]{1,0:T(8,128)} %broadcast_in_dim.11.sign_ref.refs_4_), custom_call_target="tpu_custom_call" | custom-call | flops 32768000000 | bytes 32768000 | tf_op jit(solution)/shard_map/synth/pallas_call | solution.py:363
  90.8 17.2 %all-to-all-done.1.refs_0_ = bf16[16,2,40,1280]{3,2,1,0:T(8,128)(2,1)} async-done(((bf16[16,2,40,1280]{3,2,1,0:T(8,128)(2,1)}), bf16[16,2,40,1280]{3,2,1,0:T(8,128)(2,1)}, u32[]{:S(2)}, u32[]{:S(2)}) %all-to-all-start.1) | async-done | bytes 3276832 | tf_op jit(solution)/shard_map/all_to_all | solution.py:442
  108.0 4.7 %all-to-all-start = ((bf16[16,2,40,1280]{3,2,1,0:T(8,128)(2,1)}), bf16[16,2,40,1280]{3,2,1,0:T(8,128)(2,1)}, u32[]{:S(2)}, u32[]{:S(2)}) async-start(bf16[16,2,40,1280]{3,2,1,0:T(8,128)(2,1)} %synth.2), calls=%async_computation | async-start | bytes 6553600 | tf_op jit(solution)/shard_map/all_to_all | solution.py:442
  113.0 1.6 copy-done
  114.9 3.2 pad_maximum_fusion.2
  118.1 40.3 %fourier.2 = (bf16[16,2,40,1280]{3,2,1,0:T(8,128)(2,1)}, f32[1280,640]{1,0:T(8,128)}, f32[1280,640]{1,0:T(8,128)}) custom-call(bf16[16,2,40,1280]{3,2,1,0:T(8,128)(2,1)} %all-to-all-done.1.refs_0_, bf16[5,512,640]{2,1,0:T(8,128)(2,1)} %pad_maximum_fusion.refs_1_, bf16[5,512,640]{2,1,0:T(8,128)(2,1)} %pad_maximum_fusion.1.refs_2_, ...), custom_call_target="tpu_custom_call" | custom-call | flops 41943040000 | bytes 26214400 | tf_op jit(solution)/shard_map/fourier/pallas_call | solution.py:417
  158.4 28.7 %all-to-all-done.refs_0_ = bf16[16,2,40,1280]{3,2,1,0:T(8,128)(2,1)} async-done(((bf16[16,2,40,1280]{3,2,1,0:T(8,128)(2,1)}), bf16[16,2,40,1280]{3,2,1,0:T(8,128)(2,1)}, u32[]{:S(2)}, u32[]{:S(2)}) %all-to-all-start) | async-done | bytes 3276832 | tf_op jit(solution)/shard_map/all_to_all | solution.py:442
  187.1 3.7 %all-to-all-start.3 = ((bf16[16,2,40,1280]{3,2,1,0:T(8,128)(2,1)}), bf16[16,2,40,1280]{3,2,1,0:T(8,128)(2,1)S(1)}, u32[]{:S(2)}, u32[]{:S(2)}) async-start(bf16[16,2,40,1280]{3,2,1,0:T(8,128)(2,1)} %get-tuple-element.19), calls=%async_computation.3 | async-start | bytes 6553600 | tf_op jit(solution)/shard_map/all_to_all | solution.py:442
  191.6 41.1 %fourier.3 = (bf16[16,2,40,1280]{3,2,1,0:T(8,128)(2,1)}, f32[1280,640]{1,0:T(8,128)}, f32[1280,640]{1,0:T(8,128)}) custom-call(bf16[16,2,40,1280]{3,2,1,0:T(8,128)(2,1)} %all-to-all-done.refs_0_, bf16[5,512,640]{2,1,0:T(8,128)(2,1)} %pad_maximum_fusion.refs_1_, ...), custom_call_target="tpu_custom_call", output_to_operand_aliasing={{1}: (9, {}), {2}: (10, {})} | custom-call | flops 41943040000 | bytes 26214400 | tf_op jit(solution)/shard_map/fourier/pallas_call | solution.py:417
  232.6 32.8 %all-to-all-done.3.refs_1_ = bf16[16,2,40,1280]{3,2,1,0:T(8,128)(2,1)S(1)} async-done(((bf16[16,2,40,1280]{3,2,1,0:T(8,128)(2,1)}), bf16[16,2,40,1280]{3,2,1,0:T(8,128)(2,1)S(1)}, u32[]{:S(2)}, u32[]{:S(2)}) %all-to-all-start.3) | async-done | bytes 3276832 | tf_op jit(solution)/shard_map/all_to_all | solution.py:442
  265.4 1.7 copy-done.3
  267.2 4.7 %all-to-all-start.2 = ((bf16[16,2,40,1280]{3,2,1,0:T(8,128)(2,1)}), bf16[16,2,40,1280]{3,2,1,0:T(8,128)(2,1)}, u32[]{:S(2)}, u32[]{:S(2)}) async-start(bf16[16,2,40,1280]{3,2,1,0:T(8,128)(2,1)} %get-tuple-element.18), calls=%async_computation.2 | async-start | bytes 6553600 | tf_op jit(solution)/shard_map/all_to_all | solution.py:442
  271.9 3.8 %fusion.11 = f32[80,1280]{1,0:T(8,128)S(1)} fusion(f32[1280,640]{1,0:T(8,128)} %get-tuple-element.20, s32[640]{0:T(1024)S(1)} %add_select_fusion.2, s32[80]{0:T(128)S(1)} %broadcast_select_fusion.1), kind=kOutput, calls=%fused_computation.31 | convolution fusion | flops 786483200 | bytes 3689280 | tf_op jit(solution)/shard_map/dot_general | solution.py:474
  275.7 1.7 broadcast_select_fusion
  277.5 1.6 collective-permute-start
  279.1 9.9 %collective-permute-done = f32[80,1280]{1,0:T(8,128)S(1)} collective-permute-done((f32[80,1280]{1,0:T(8,128)S(1)}, f32[80,1280]{1,0:T(8,128)S(1)}, u32[]{:S(2)}, u32[]{:S(2)}) %collective-permute-start) | collective-permute-done | bytes 409632 | tf_op jit(solution)/shard_map/ppermute | solution.py:487
  291.2 25.5 %analyse.2.refs_5_ = f32[32,2,40,640]{3,2,1,0:T(8,128)} custom-call(s32[40]{0:T(128)} %get-tuple-element.31.orders_ref.refs_0_, bf16[16,2,40,1280]{3,2,1,0:T(8,128)(2,1)} %copy-done.3, f32[1,640]{1,0:T(1,128)} %broadcast_in_dim.10.root_ref.refs_2_, bf16[320,2,40,1280]{3,2,1,0:T(8,128)(2,1)} %bitcast.42, f32[40,640]{1,0:T(8,128)} %broadcast_in_dim.11.sign_ref.refs_4_), custom_call_target="tpu_custom_call" | custom-call | flops 32768000000 | bytes 32768000 | tf_op jit(solution)/shard_map/analyse/pallas_call | solution.py:386
  316.7 29.6 %all-to-all-done.2.refs_1_ = bf16[16,2,40,1280]{3,2,1,0:T(8,128)(2,1)} async-done(((bf16[16,2,40,1280]{3,2,1,0:T(8,128)(2,1)}), bf16[16,2,40,1280]{3,2,1,0:T(8,128)(2,1)}, u32[]{:S(2)}, u32[]{:S(2)}) %all-to-all-start.2) | async-done | bytes 3276832 | tf_op jit(solution)/shard_map/all_to_all | solution.py:442
  346.3 25.6 %analyse.3 = f32[32,2,40,640]{3,2,1,0:T(8,128)} custom-call(s32[40]{0:T(128)} %get-tuple-element.31.orders_ref.refs_0_, bf16[16,2,40,1280]{3,2,1,0:T(8,128)(2,1)} %all-to-all-done.2.refs_1_, f32[1,640]{1,0:T(1,128)} %broadcast_in_dim.10.root_ref.refs_2_, bf16[320,2,40,1280]{3,2,1,0:T(8,128)(2,1)} %bitcast.43, ...), custom_call_target="tpu_custom_call", output_to_operand_aliasing={{}: (5, {})} | custom-call | flops 32768000000 | bytes 32768000 | tf_op jit(solution)/shard_map/analyse/pallas_call | solution.py:386
  (52 shorter events, 13.2 us)
Async XLA Ops:
  25.7 7.6 %copy-start.4 = (f32[80,2560]{1,0:T(8,128)S(1)}, f32[80,2560]{1,0:T(8,128)}, u32[]{:S(2)}) copy-start(f32[80,2560]{1,0:T(8,128)} %param.10) | copy-start | bytes 2457604
  25.7 82.2 %all-to-all-start.1 = ((bf16[16,2,40,1280]{3,2,1,0:T(8,128)(2,1)}), bf16[16,2,40,1280]{3,2,1,0:T(8,128)(2,1)}, u32[]{:S(2)}, u32[]{:S(2)}) async-start(bf16[16,2,40,1280]{3,2,1,0:T(8,128)(2,1)} %synth.3), calls=%async_computation.1 | async-start | bytes 6553600 | tf_op jit(solution)/shard_map/all_to_all | solution.py:442
  33.3 2.6 copy-start.8
  34.0 3.4 copy-start.2
  37.2 2.9 copy-start.6
  37.2 2.9 copy-start.7
  44.6 7.5 %slice-start = ((f32[2560,80]{0,1:T(8,128)}), f32[1,80]{0,1:T(8,128)S(1)}, s32[]{:S(2)}) async-start(f32[2560,80]{0,1:T(8,128)} %copy-done.2), calls=%async_computation.4 | async-start | bytes 81920 | tf_op jit(solution)/shard_map/slice | solution.py:454
  57.0 4.1 %copy-start.9 = (f32[32]{0:T(128)S(1)}, f32[32]{0:T(128)}, u32[]{:S(2)}) copy-start(f32[32]{0:T(128)} %param.11) | copy-start | bytes 388
  90.8 21.8 %copy-start.1 = (f32[640,1280]{1,0:T(8,128)S(1)}, f32[640,1280]{1,0:T(8,128)}, u32[]{:S(2)}) copy-start(f32[640,1280]{1,0:T(8,128)} %copy.19) | copy-start | bytes 9830404
  108.0 79.1 %all-to-all-start = ((bf16[16,2,40,1280]{3,2,1,0:T(8,128)(2,1)}), bf16[16,2,40,1280]{3,2,1,0:T(8,128)(2,1)}, u32[]{:S(2)}, u32[]{:S(2)}) async-start(bf16[16,2,40,1280]{3,2,1,0:T(8,128)(2,1)} %synth.2), calls=%async_computation | async-start | bytes 6553600 | tf_op jit(solution)/shard_map/all_to_all | solution.py:442
  112.6 1.9 copy-start
  187.1 78.3 %all-to-all-start.3 = ((bf16[16,2,40,1280]{3,2,1,0:T(8,128)(2,1)}), bf16[16,2,40,1280]{3,2,1,0:T(8,128)(2,1)S(1)}, u32[]{:S(2)}, u32[]{:S(2)}) async-start(bf16[16,2,40,1280]{3,2,1,0:T(8,128)(2,1)} %get-tuple-element.19), calls=%async_computation.3 | async-start | bytes 6553600 | tf_op jit(solution)/shard_map/all_to_all | solution.py:442
  265.4 1.7 copy-start.3
  267.2 79.1 %all-to-all-start.2 = ((bf16[16,2,40,1280]{3,2,1,0:T(8,128)(2,1)}), bf16[16,2,40,1280]{3,2,1,0:T(8,128)(2,1)}, u32[]{:S(2)}, u32[]{:S(2)}) async-start(bf16[16,2,40,1280]{3,2,1,0:T(8,128)(2,1)} %get-tuple-element.18), calls=%async_computation.2 | async-start | bytes 6553600 | tf_op jit(solution)/shard_map/all_to_all | solution.py:442
  271.9 3.8 %copy-start.5 = (f32[1280,640]{1,0:T(8,128)S(1)}, f32[1280,640]{1,0:T(8,128)}, u32[]{:S(2)}) copy-start(f32[1280,640]{1,0:T(8,128)} %get-tuple-element.21) | copy-start | bytes 9830404
  277.5 11.5 %collective-permute-start = (f32[80,1280]{1,0:T(8,128)S(1)}, f32[80,1280]{1,0:T(8,128)S(1)}, u32[]{:S(2)}, u32[]{:S(2)}) collective-permute-start(f32[80,1280]{1,0:T(8,128)S(1)} %get-tuple-element.42), channel_id=1, source_target_pairs={{0,1},{1,0},{2,3},{3,2},{4,5},{5,4},{6,7},{7,6},{8,9},{9,8},{10,11... | collective-permute-start | bytes 1228808 | tf_op jit(solution)/shard_map/ppermute | solution.py:487
